TPU v7x, 256 devices: a whole 4x4x8 slice. The times are simulated.
256 devices in a mesh: dp: 32 (over x, z_lo, core), expert: 8 (over y, z_hi).
Axes of the slice: x: 4, y: 4, z: 8 (z_hi: 2, z_lo: 4; z = z_hi * 4 + z_lo), core: 2. Of those that a mesh axis runs over, the one named last changes fastest.
Arguments:
- grad_out: bfloat16 [131072, 3072], P(('dp', 'expert')), may hold values from -0.19921875 to 0.19921875
- expert_ids: int32 [131072, 2], P(('dp', 'expert')), may hold values from 0 to 7, all different within a row; in each aligned block of 512 rows (0 to 511, 512 to 1023, ...) at most 192 rows name the same one
- gate_probs: float32 [131072, 2], P(('dp', 'expert')), may hold values from 0.1 to 1
- saved_gate: bfloat16 [49152, 8, 1024], P('dp', 'expert'), may hold values from -6 to 6
- saved_up: bfloat16 [49152, 8, 1024], P('dp', 'expert'), may hold values from -6 to 6
- master: float32 [8, 1024, 3072], P('expert', 'dp')
- moment_one: float32 [8, 1024, 3072], P('expert', 'dp'), may hold values from -2 to 2
- moment_two: float32 [8, 1024, 3072], P('expert', 'dp'), may hold values from 0.05 to 1
Outputs:
- new_master: float32 [8, 1024, 3072], P('expert', 'dp')
- new_moment_one: float32 [8, 1024, 3072], P('expert', 'dp')
- new_moment_two: float32 [8, 1024, 3072], P('expert', 'dp')
- new_weights: float32 [8, 1024, 3072], P('expert')
Inputs may be any that keep to these rules, and one draw needn't show every extreme that they name: `expert_ids`: in each aligned block of 512 rows (the tokens of one device) no expert is named by more than 192 rows, a bound that some block reaches.
All inputs are finite; a program needn't handle non-finite values.
Results may differ from a plain program's by a relative error of at most 0.00035.
Values may be sent and summed in bfloat16 or wider, within the bound.
A program may use at most 128 MiB of HBM per device.

v0:
```python
import jax
import jax.numpy as jnp
from jax import lax
from jax.sharding import PartitionSpec as P


def local(grad_out, expert_ids, gate_probs, saved_gate, saved_up, master, moment_one, moment_two):
    tok_rows = grad_out.shape[0]
    cap_rows = tok_rows * 3 // 8
    hit = expert_ids == 0
    chosen = jnp.any(hit, axis=1)
    weight = jnp.sum(jnp.where(hit, gate_probs, jnp.float32(0.0)), axis=1)
    slot = jnp.cumsum(chosen.astype(jnp.int32)) - 1
    scaled = (weight[:, None] * grad_out.astype(jnp.float32)).astype(jnp.bfloat16)
    places = jnp.arange(cap_rows, dtype=jnp.int32)
    placing = ((slot[None, :] == places[:, None]) & chosen[None, :]).astype(jnp.bfloat16)
    dispatched = jnp.dot(placing, scaled, preferred_element_type=jnp.float32).astype(jnp.bfloat16)
    slot_rows = saved_gate.shape[0]
    width = saved_gate.shape[2]
    gate_part = saved_gate.reshape(slot_rows, width)
    up_part = saved_up.reshape(slot_rows, width)
    hidden = (jax.nn.silu(gate_part.astype(jnp.float32)) * up_part.astype(jnp.float32)).astype(
        jnp.bfloat16
    )
    contract = (((0,), (0,)), ((), ()))
    everyone = lax.all_gather(dispatched, "expert", axis=0, tiled=True)
    total = lax.dot_general(hidden, everyone, contract, preferred_element_type=jnp.float32)
    grad_slice = lax.psum_scatter(total, "dp", scatter_dimension=0, tiled=True)
    grad = grad_slice.reshape(master.shape)
    new_one = 0.9 * moment_one + 0.1 * grad
    new_two = 0.95 * moment_two + 0.05 * grad * grad
    step = new_one / (1.0 - 0.9**20) / (jnp.sqrt(new_two / (1.0 - 0.95**20)) + 1e-08)
    wrms = jnp.sqrt(jnp.mean(master * master, axis=-1, keepdims=True) + 1e-06)
    srms = jnp.sqrt(jnp.mean(step * step, axis=-1, keepdims=True) + 1e-06)
    factor = jnp.minimum(1.0, 0.02 * wrms / (0.01 * srms))
    new_master = master - 0.01 * factor * step
    gathered = lax.all_gather(new_master, "dp", axis=1, tiled=True)
    return (new_master, new_one, new_two, gathered)


def solution(mesh):
    return jax.shard_map(
        local,
        mesh=mesh,
        in_specs=(
            P(("dp", "expert"), None),
            P(("dp", "expert"), None),
            P(("dp", "expert"), None),
            P("dp", "expert", None),
            P("dp", "expert", None),
            P("expert", "dp", None),
            P("expert", "dp", None),
            P("expert", "dp", None),
        ),
        out_specs=(
            P("expert", "dp", None),
            P("expert", "dp", None),
            P("expert", "dp", None),
            P("expert", None, None),
        ),
        check_vma=False,
    )
```

profile of v0, /device:TPU:1, one launch (start us, length us, event | category | flops | bytes accessed | tf_op | source)
XLA Modules:
  0.0 490.4 jit_solution(2230872570642506750)
XLA Ops:
  7.2 0.0 all-gather.3.cloned.1.call-start
  7.2 0.9 fusion.17
  8.1 0.3 reduce-window.9
  8.4 0.1 slice.7
  8.5 0.1 slice_reduce_fusion
  8.6 0.1 add_bitcast_fusion
  8.7 0.7 select_reduce_fusion
  9.4 3.8 convolution_convert_fusion
  13.2 0.0 all-gather.3.cloned.1.call-update
  13.3 0.0 reduce-scatter.2.cloned.1.call-start
  13.3 193.8 %all-gather.3.cloned.1.call-done = bf16[1536,3072]{1,0:T(8,128)(2,1)} async-done(((bf16[192,3072]{1,0:T(8,128)(2,1)}), bf16[1536,3072]{1,0:T(8,128)(2,1)}) %all-gather.3.cloned.1.call-update) | async-done | bytes 9437200 | tf_op jit(solution)/shard_map/all_gather | solution.py:26
  207.1 17.5 %fusion.5 = f32[1024,3072]{1,0:T(8,128)} fusion(bf16[1536,3072]{1,0:T(8,128)(2,1)} %all-gather.3.cloned.1.call-done, bf16[1536,1,1024]{2,0,1:T(8,128)(2,1)S(1)} %copy-done.5, bf16[1536,1,1024]{2,0,1:T(8,128)(2,1)} %param.11), kind=kOutput, calls=%fused_computation.9 | convolution fusion | flops 9676259328 | bytes 28311552 | tf_op jit(solution)/shard_map/dot_general | solution.py:27
  224.6 0.0 reduce-scatter.2.cloned.1.call-update
  224.7 0.0 all-gather.5.cloned.1.call-start
  224.7 0.9 copy-done
  225.6 0.1 multiply_reduce_fusion.1
  225.8 164.9 %reduce-scatter.2.cloned.1.call-done = f32[32,3072]{1,0:T(8,128)} async-done(((f32[1024,3072]{1,0:T(8,128)}), f32[32,3072]{1,0:T(8,128)}) %reduce-scatter.2.cloned.1.call-update) | async-done | bytes 393232 | tf_op jit(solution)/shard_map/reduce_scatter | solution.py:28
  390.7 0.0 copy-done.4
  390.7 1.4 multiply_reduce_fusion
  392.1 0.0 copy-start.2
  392.1 1.0 multiply_subtract_fusion
  393.1 0.0 all-gather.5.cloned.1.call-update
  393.1 79.8 %all-gather.5.cloned.1.call-done = f32[1,1024,3072]{2,1,0:T(8,128)} async-done(((f32[1,32,3072]{2,1,0:T(8,128)}), f32[1,1024,3072]{2,1,0:T(8,128)}) %all-gather.5.cloned.1.call-update) | async-done | bytes 12582928 | tf_op jit(solution)/shard_map/all_gather | solution.py:37
  472.9 11.0 %copy.13 = f32[1,1024,3072]{2,1,0:T(8,128)} copy(f32[1,1024,3072]{2,1,0:T(8,128)} %all-gather.5.cloned.1.call-done) | data formatting | bytes 25165824
  (12 shorter events, 0.1 us)
Async XLA Ops:
  7.2 200.0 %copy-start.5 = (bf16[1536,1,1024]{2,0,1:T(8,128)(2,1)S(1)}, bf16[1536,1,1024]{2,0,1:T(8,128)(2,1)}, u32[]{:S(2)}) copy-start(bf16[1536,1,1024]{2,0,1:T(8,128)(2,1)} %param.12) | copy-start | bytes 9437188
  7.2 200.0 %all-gather.3.cloned.1.call-start = ((), (), s32[]{:S(2)}) async-start(), calls=%async_computation.1 | async-start | bytes 10616832 | tf_op jit(solution)/shard_map/all_gather | solution.py:26
  13.3 377.4 %reduce-scatter.2.cloned.1.call-start = ((), (), s32[]{:S(2)}) async-start(), calls=%async_computation.2 | async-start | bytes 12976128 | tf_op jit(solution)/shard_map/reduce_scatter | solution.py:28
  224.6 1.0 copy-start
  224.6 166.0 %copy-start.3 = (f32[1,32,3072]{2,1,0:T(8,128)S(1)}, f32[1,32,3072]{2,1,0:T(8,128)}, u32[]{:S(2)}) copy-start(f32[1,32,3072]{2,1,0:T(8,128)} %param.14) | copy-start | bytes 1179652
  224.6 166.0 %copy-start.4 = (f32[1,32,3072]{2,1,0:T(8,128)S(1)}, f32[1,32,3072]{2,1,0:T(8,128)}, u32[]{:S(2)}) copy-start(f32[1,32,3072]{2,1,0:T(8,128)} %param.15) | copy-start | bytes 1179652
  224.7 248.2 %all-gather.5.cloned.1.call-start = ((), (), s32[]{:S(2)}) async-start(), calls=%async_computation.3 | async-start | bytes 12976128 | tf_op jit(solution)/shard_map/all_gather | solution.py:37
  392.0 91.9 %copy-start.1 = (f32[1,32,3072]{2,1,0:T(8,128)}, f32[1,32,3072]{2,1,0:T(8,128)S(1)}, u32[]{:S(2)}) copy-start(f32[1,32,3072]{2,1,0:T(8,128)S(1)} %get-tuple-element.12) | copy-start | bytes 1179652
  392.1 91.9 %copy-start.2 = (f32[1,32,3072]{2,1,0:T(8,128)}, f32[1,32,3072]{2,1,0:T(8,128)S(1)}, u32[]{:S(2)}) copy-start(f32[1,32,3072]{2,1,0:T(8,128)S(1)} %get-tuple-element.13) | copy-start | bytes 1179652
Sparse Core Ops, SparseCore 0:
  13.4 193.7 all-gather.2
  224.8 165.8 reduce-scatter.1
  393.2 79.6 all-gather.4
where the time goes:
time: 491 us; the launch traced here: 490 us
  waiting for transfers between devices  439 us (89%)
  matrix products  21.3 us (4%)
  between operations  13.8 us (3%)
  local copies, waits for them, and re-layouts  12.1 us (2%)
    all_gather x1, waiting for transfers between devices, local(): everyone = lax.all_gather(dispatched, 'expert', axis=0, tiled=True)  194 us
    reduce_scatter x1, waiting for transfers between devices, local(): grad_slice = lax.psum_scatter(total, 'dp', scatter_dimension=0, tiled=True)  165 us
    all_gather x1, waiting for transfers between devices, local(): gathered = lax.all_gather(new_master, 'dp', axis=1, tiled=True)  79.8 us
    dot_general x1, matrix products, local(): lax.dot_general(hidden, everyone, contract, preferred_element_type=jnp.fl...  17.5 us
    unnamed x13, local copies, waits for them, and re-layouts  11.9 us
  transfers between devices with their start and end apart: 3, of which 3 were waited for; matrix products, arithmetic and copies ran while one was open for 0% of the time, Pallas kernels for 0%

commit v1 on v0

--- a/solution.py
+++ b/solution.py
@@ -34,7 +34,9 @@
     srms = jnp.sqrt(jnp.mean(step * step, axis=-1, keepdims=True) + 1e-06)
     factor = jnp.minimum(1.0, 0.02 * wrms / (0.01 * srms))
     new_master = master - 0.01 * factor * step
-    gathered = lax.all_gather(new_master, "dp", axis=1, tiled=True)
+    gathered = jnp.concatenate(
+        lax.all_to_all(jnp.stack([new_master] * lax.axis_size("dp")), "dp", 0, 0), axis=1
+    )
     return (new_master, new_one, new_two, gathered)
 
 

time: 491 us -> 695 us (1.42)
  blocking collectives: 0 us -> 283 us
  waiting for transfers between devices: 439 us -> 358 us
    all_to_all x0 -> x1, blocking collectives: none -> 283 us  [local(): lax.all_to_all(jnp.stack([new_master] * lax.axis_size('dp')), 'dp', 0, 0)]
    all_gather x1 -> x0, waiting for transfers between devices: 79.8 us -> none  [local(): gathered = lax.all_gather(new_master, 'dp', axis=1, tiled=True)]
  transfers between devices with their start and end apart: 3 -> 2, of which waited for: 3 -> 2; matrix products, arithmetic and copies ran while one was open for 0% -> 0% of each run, Pallas kernels for 0% -> 0%
where the time goes in v1:
time: 695 us
  waiting for transfers between devices  358 us (52%)
  blocking collectives  283 us (41%)
  matrix products  21.3 us (3%)
  between operations  14.1 us (2%)
  local copies, waits for them, and re-layouts  13.7 us (2%)
    all_to_all x1, blocking collectives, local(): lax.all_to_all(jnp.stack([new_master] * lax.axis_size('dp')), 'dp', 0, 0)  283 us
    all_gather x1, waiting for transfers between devices, local(): everyone = lax.all_gather(dispatched, 'expert', axis=0, tiled=True)  194 us
    reduce_scatter x1, waiting for transfers between devices, local(): grad_slice = lax.psum_scatter(total, 'dp', scatter_dimension=0, tiled=True)  165 us
    dot_general x1, matrix products, local(): lax.dot_general(hidden, everyone, contract, preferred_element_type=jnp.fl...  17.5 us
  transfers between devices with their start and end apart: 2, of which 2 were waited for; matrix products, arithmetic and copies ran while one was open for 0% of the time, Pallas kernels for 0%

profile of v1, /device:TPU:1, one launch (start us, length us, event | category | flops | bytes accessed | tf_op | source)
XLA Modules:
  0.0 694.6 jit_solution(12441485159932107662)
XLA Ops:
  7.2 0.0 all-gather.2.cloned.1.call-start
  7.2 0.9 fusion.17
  8.1 0.3 reduce-window.9
  8.4 0.1 slice.7
  8.5 0.1 slice_reduce_fusion
  8.6 0.1 add_bitcast_fusion
  8.7 0.7 select_reduce_fusion
  9.4 3.8 convolution_convert_fusion
  13.2 0.0 all-gather.2.cloned.1.call-update
  13.3 0.0 reduce-scatter.2.cloned.1.call-start
  13.3 193.8 %all-gather.2.cloned.1.call-done = bf16[1536,3072]{1,0:T(8,128)(2,1)} async-done(((bf16[192,3072]{1,0:T(8,128)(2,1)}), bf16[1536,3072]{1,0:T(8,128)(2,1)}) %all-gather.2.cloned.1.call-update) | async-done | bytes 9437200 | tf_op jit(solution)/shard_map/all_gather | solution.py:26
  207.1 17.5 %fusion.5 = f32[1024,3072]{1,0:T(8,128)} fusion(bf16[1536,3072]{1,0:T(8,128)(2,1)} %all-gather.2.cloned.1.call-done, bf16[1536,1,1024]{2,0,1:T(8,128)(2,1)S(1)} %copy-done.6, bf16[1536,1,1024]{2,0,1:T(8,128)(2,1)} %param.11), kind=kOutput, calls=%fused_computation.9 | convolution fusion | flops 9676259328 | bytes 28311552 | tf_op jit(solution)/shard_map/dot_general | solution.py:27
  224.7 0.0 reduce-scatter.2.cloned.1.call-update
  224.7 1.0 copy-done.1
  225.6 0.1 multiply_reduce_fusion.1
  225.8 164.6 %reduce-scatter.2.cloned.1.call-done = f32[32,3072]{1,0:T(8,128)} async-done(((f32[1024,3072]{1,0:T(8,128)}), f32[32,3072]{1,0:T(8,128)}) %reduce-scatter.2.cloned.1.call-update) | async-done | bytes 393232 | tf_op jit(solution)/shard_map/reduce_scatter | solution.py:28
  390.4 0.0 copy-done.5
  390.4 1.4 multiply_reduce_fusion
  391.8 0.0 copy-start.3
  391.8 0.2 multiply_subtract_fusion
  392.0 0.0 copy-start
  392.0 1.6 stack.2
  393.6 283.1 %all_to_all.5 = f32[32,1,32,3072]{3,2,1,0:T(8,128)} all-to-all(f32[32,1,32,3072]{3,2,1,0:T(8,128)S(1)} %stack.2), channel_id=1, replica_groups=mesh['dp'=32,'expert'=8] {'dp'}, dimensions={0} | all-to-all | bytes 25165824 | tf_op jit(solution)/shard_map/all_to_all | solution.py:38
  676.8 11.0 %copy.13 = f32[1,1024,3072]{2,1,0:T(8,128)} copy(f32[1,1024,3072]{2,1,0:T(8,128)} %bitcast.27) | data formatting | bytes 25165824
  (13 shorter events, 0.1 us)
Async XLA Ops:
  7.2 200.0 %copy-start.6 = (bf16[1536,1,1024]{2,0,1:T(8,128)(2,1)S(1)}, bf16[1536,1,1024]{2,0,1:T(8,128)(2,1)}, u32[]{:S(2)}) copy-start(bf16[1536,1,1024]{2,0,1:T(8,128)(2,1)} %param.12) | copy-start | bytes 9437188
  7.2 200.0 %all-gather.2.cloned.1.call-start = ((), (), s32[]{:S(2)}) async-start(), calls=%async_computation.2 | async-start | bytes 10616832 | tf_op jit(solution)/shard_map/all_gather | solution.py:26
  13.3 377.1 %reduce-scatter.2.cloned.1.call-start = ((), (), s32[]{:S(2)}) async-start(), calls=%async_computation.3 | async-start | bytes 12976128 | tf_op jit(solution)/shard_map/reduce_scatter | solution.py:28
  224.6 1.0 copy-start.1
  224.6 165.7 %copy-start.4 = (f32[1,32,3072]{2,1,0:T(8,128)S(1)}, f32[1,32,3072]{2,1,0:T(8,128)}, u32[]{:S(2)}) copy-start(f32[1,32,3072]{2,1,0:T(8,128)} %param.14) | copy-start | bytes 1179652
  224.6 165.7 %copy-start.5 = (f32[1,32,3072]{2,1,0:T(8,128)S(1)}, f32[1,32,3072]{2,1,0:T(8,128)}, u32[]{:S(2)}) copy-start(f32[1,32,3072]{2,1,0:T(8,128)} %param.15) | copy-start | bytes 1179652
  391.7 1.8 copy-start.2
  391.8 1.8 copy-start.3
  392.0 1.6 copy-start
Sparse Core Ops, SparseCore 0:
  13.4 193.7 all-gather.1
  224.8 165.5 reduce-scatter.1
